TPU v7x, 768 devices: a whole 4x8x12 slice. The times are simulated.
768 devices in a mesh: cuts: 24 (over x_hi, z), group: 32 (over y, x_lo, core).
Axes of the slice: x: 4 (x_hi: 2, x_lo: 2; x = x_hi * 2 + x_lo), y: 8, z: 12, core: 2. Of those that a mesh axis runs over, the one named last changes fastest.
Arguments:
- radiation: float32 [768, 2, 128, 128], P(('cuts', 'group')), may hold values from -6 to 6
- phases: float32 [768, 16, 128], P(('cuts', 'group')), may hold values from -3.140625 to 3.140625
- energy: float32 [768, 16, 128], P(('cuts', 'group')), may hold values from -5 to 5
- pixels: int32 [768, 16, 128], P(('cuts', 'group')), may hold values from 0 to 16383
- destination: int32 [768, 16], P(('cuts', 'group')), may hold values from 0 to 23, as said below
- propagator: float32 [2, 128, 128], replicated, may hold values from -1 to 1
- transmit: float32 [2, 768], replicated, may hold values from -1 to 1
Outputs:
- radiation_out: float32 [768, 2, 128, 128], P(('cuts', 'group'))
Inputs may be any that keep to these rules, and one draw needn't show every extreme that they name: `destination`: the blocks of one slice go to exactly 8 different cuts, 2 blocks to each; in every draw some cut receives 2 blocks from every slice of the same position within a cut.
All inputs are finite; a program needn't handle non-finite values.
Results may differ from a plain program's by a relative error of at most 0.0011.
Values sent between devices are 32-bit elements; how exact they have to be, the bound alone decides.
A program may use at most 32 MiB of HBM per device.

v0:
```python
import functools
import math

import jax
import jax.numpy as jnp
from jax import lax
from jax.experimental import pallas as pl
from jax.experimental.pallas import tpu as pltpu
from jax.sharding import PartitionSpec as P

KICK_RATE = 0.5
PHASE_RATE = 1.0
EMIT_RATE = 0.5
F32 = jnp.float32
BF16 = jnp.bfloat16
MESH = pl.DeviceIdType.MESH
ROWS = 8
HALF = 4


def iota(shape, dim):
    return lax.broadcasted_iota(jnp.int32, shape, dim)


def split(x):
    high = x.astype(BF16)
    return high, (x - high.astype(F32)).astype(BF16)


def dot(a, b):
    return jnp.dot(a, b, preferred_element_type=F32)


def dot_nt(a, b):
    return lax.dot_general(a, b, (((1,), (1,)), ((), ())), preferred_element_type=F32)


def dot_exact(a, b):
    return jnp.dot(a, b, precision=lax.Precision.HIGHEST, preferred_element_type=F32)


def turns(product, total):
    whole = jnp.floor((product + 0.5) * (1.0 / total))
    angle = (product - whole * total) * (2.0 * math.pi / total)
    return jnp.cos(angle), jnp.sin(angle)


def stack2(a, b, c, d):
    return jnp.concatenate(
        [jnp.concatenate([a, b], axis=1), jnp.concatenate([c, d], axis=1)], axis=0
    )


def triple(matrix):
    high, low = split(matrix)
    return jnp.concatenate([high, high, low], axis=1)


def apply_triple(packed, data):
    high, low = split(data)
    return dot(packed, jnp.concatenate([high, low, high], axis=0))


def kernel(
    n_cuts, n_group, grid, blocks, width,
    radiation, phases, energy, pixels, destination, propagator, transmit,
    out,
    field, prop_hi, prop_lo, cut_fwd, cut_inv, mid_op,
    slip_a, got_a, slip_p, got_p, slip_b, got_b,
    pix, onehot, read, weight, source,
    send1, recv1, send2, recv2, send3, recv3, send4, recv4, send_e, recv_e,
    send_sems, recv_sems,
):
    c = lax.axis_index("cuts")
    g = lax.axis_index("group")
    total = n_cuts * n_group
    me = c * n_group + g
    n_active = grid // ROWS
    lane = c % 3
    active = lane < 2
    idle_cut = c - lane + 2
    half_group = n_group // 2
    my_active = 2 * (c // 3) + lane
    owner = jnp.where(active, c, c - 2 + g // half_group)
    unit = jnp.where(active, g, n_group + g % half_group)
    units = 2 * n_cuts
    many = 2 * n_cuts
    before = (me + total - 1) % total
    after = (me + 1) % total

    def repeat(count, body):
        def step(i, carry):
            body(i)
            return carry
        lax.fori_loop(0, count, step, 0)

    barrier = pltpu.get_barrier_semaphore()

    def hello(cc, gg):
        pl.semaphore_signal(barrier, inc=1, device_id=(cc, gg), device_id_type=MESH)

    hello(before // n_group, before % n_group)
    hello(after // n_group, after % n_group)
    repeat(n_cuts - 1, lambda i: hello((c + 1 + i) % n_cuts, g))

    @pl.when(active)
    def _():
        repeat(n_group - 1, lambda i: hello(c, (g + 1 + i) % n_group))
        repeat(half_group, lambda i: hello(idle_cut, half_group * lane + i))

    @pl.when(jnp.logical_not(active))
    def _():
        repeat(n_group, lambda i: hello(owner, (g + i) % n_group))

    ahead_group = (g + 3) % n_group
    behind_group = (g + n_group - 3) % n_group
    repeat(n_cuts, lambda i: hello((c + i) % n_cuts, ahead_group))
    repeat(n_cuts, lambda i: hello((c + i) % n_cuts, behind_group))

    def meet():
        greeted = 2 + (n_cuts - 1) + 2 * n_cuts

        @pl.when(active)
        def _():
            pl.semaphore_wait(barrier, greeted + n_group - 1 + half_group)

        @pl.when(jnp.logical_not(active))
        def _():
            pl.semaphore_wait(barrier, greeted + n_group)

    def remote(stage, src, dst, cc, gg):
        return pltpu.make_async_remote_copy(
            src_ref=src, dst_ref=dst, send_sem=send_sems.at[stage], recv_sem=recv_sems.at[stage],
            device_id=(cc, gg), device_id_type=MESH,
        )

    def push(stage, src, dst, cc, gg):
        mine = jnp.logical_and(cc == c, gg == g)

        @pl.when(mine)
        def _():
            pltpu.make_async_copy(src, dst, recv_sems.at[stage]).start()

        @pl.when(jnp.logical_not(mine))
        def _():
            remote(stage, src, dst, cc, gg).start()

    def arrived(stage, ref):
        remote(stage, ref, ref, c, g).wait_recv()

    def sent(stage, ref):
        remote(stage, ref, ref, c, g).wait_send()

    def rows_of(ref, index, count):
        return ref.at[pl.ds(pl.multiple_of(index * count, count), count)]

    def chunk_of(count):
        return 8 if count % 8 == 0 else count

    def mark(count):
        chunk = chunk_of(count)
        def body(i):
            first = pl.multiple_of(i * chunk, chunk)
            cells = pix[pl.ds(first, chunk), :] & (grid - 1)
            hot = [
                (iota((grid, width), 0) == jnp.broadcast_to(cells[b:b + 1], (grid, width))).astype(F32).astype(BF16)
                for b in range(chunk)
            ]
            onehot[i] = jnp.concatenate(hot, axis=1)
        repeat(count // chunk, body)

    def look(count):
        chunk = chunk_of(count)
        low = field[...].astype(BF16)
        shift = grid.bit_length() - 1
        def body(i):
            first = pl.multiple_of(i * chunk, chunk)
            cells = lax.shift_right_arithmetic(pix[pl.ds(first, chunk), :], shift)
            real, imag = [], []
            for pair in range(chunk // 2):
                hot = onehot[i, :, pair * 2 * width:(pair + 1) * 2 * width]
                picked = dot(low, hot)
                for b in range(2):
                    match = iota((grid, width), 0) == jnp.broadcast_to(cells[2 * pair + b:2 * pair + b + 1], (grid, width))
                    part = picked[:, b * width:(b + 1) * width]
                    real.append(jnp.sum(jnp.where(match, part[:grid], 0.0), axis=0, keepdims=True))
                    imag.append(jnp.sum(jnp.where(match, part[grid:], 0.0), axis=0, keepdims=True))
            read[0, pl.ds(first, chunk), :] = jnp.concatenate(real, axis=0)
            read[1, pl.ds(first, chunk), :] = jnp.concatenate(imag, axis=0)
        repeat(count // chunk, body)

    def kick(count, phase, power):
        power = power - KICK_RATE * (read[0, :count] * jnp.cos(phase) - read[1, :count] * jnp.sin(phase))
        phase = phase + PHASE_RATE * power
        weight[0, :count] = jnp.cos(phase)
        weight[1, :count] = -jnp.sin(phase)
        return phase, power

    def deposit(count):
        chunk = chunk_of(count)
        shift = grid.bit_length() - 1
        source[...] = jnp.zeros_like(source)
        def body(i):
            first = pl.multiple_of(i * chunk, chunk)
            cells = lax.shift_right_arithmetic(pix[pl.ds(first, chunk), :], shift)
            real = weight[0, pl.ds(first, chunk), :]
            imag = weight[1, pl.ds(first, chunk), :]
            tops, bottoms = [], []
            for b in range(chunk):
                match = iota((grid, width), 0) == jnp.broadcast_to(cells[b:b + 1], (grid, width))
                tops.append(jnp.where(match, jnp.broadcast_to(real[b:b + 1], (grid, width)), 0.0).astype(BF16))
                bottoms.append(jnp.where(match, jnp.broadcast_to(imag[b:b + 1], (grid, width)), 0.0).astype(BF16))
            spread = jnp.concatenate([jnp.concatenate(tops, axis=1), jnp.concatenate(bottoms, axis=1)], axis=0)
            source[...] += dot_nt(spread, onehot[i])
        repeat(count // chunk, body)

    def diffract(keep):
        emitted = field[...] + EMIT_RATE * source[...]
        high, low = split(emitted)
        both = dot(prop_hi[...], jnp.concatenate([high, low], axis=1))
        left = both[:, :grid] + both[:, grid:] + dot(prop_lo[...], high)
        left = jnp.concatenate([left[:grid], left[grid:]], axis=1)
        high, low = split(left)
        result = dot_nt(high, prop_hi[...]) + dot_nt(low, prop_hi[...]) + dot_nt(high, prop_lo[...])
        return jnp.where(keep, result, 0.0)

    def set_field(result):
        field[:grid] = result[:, :grid]
        field[grid:] = result[:, grid:]

    field[:grid] = radiation[0, 0]
    field[grid:] = radiation[0, 1]
    pix[:blocks] = pixels[0]
    mark(blocks)
    look(blocks)
    phase, power = kick(blocks, phases[0], energy[0])
    slip_a[:blocks] = phase
    slip_a[blocks:2 * blocks] = power
    slip_a[2 * blocks:3 * blocks] = pixels[0].astype(F32)
    slip_a[3 * blocks:] = jnp.zeros_like(slip_a[3 * blocks:])
    slip_a[3 * blocks:3 * blocks + 1, :blocks] = destination[...].astype(F32)

    prop = stack2(propagator[0], -propagator[1], propagator[1], propagator[0])
    high, low = split(prop)
    prop_hi[...] = high
    prop_lo[...] = low
    deposit(blocks)

    meet()
    remote(0, slip_a, got_a, before // n_group, before % n_group).start()

    set_field(diffract(me != total - 1))
    shape = (n_cuts, n_cuts)
    g_real = g.astype(F32)
    cos, sin = turns((iota(shape, 1).astype(F32) * n_group + g_real) * iota(shape, 0).astype(F32), total)
    cut_fwd[...] = triple(stack2(cos, sin, -sin, cos))
    cos, sin = turns((iota(shape, 0).astype(F32) * n_group + g_real) * iota(shape, 1).astype(F32), total)
    cut_inv[...] = triple(stack2(cos, -sin, sin, cos))
    first_freq = unit // 2
    shape = (n_group, total)
    chosen = iota(shape, 1) == first_freq + n_cuts * iota(shape, 0)
    gain_real = jnp.sum(jnp.where(chosen, jnp.broadcast_to(transmit[0:1], shape), 0.0), axis=1, keepdims=True)
    gain_imag = jnp.sum(jnp.where(chosen, jnp.broadcast_to(transmit[1:2], shape), 0.0), axis=1, keepdims=True)
    shape = (n_group, n_group)
    lag_cos, lag_sin = turns((first_freq.astype(F32) + n_cuts * iota(shape, 0).astype(F32)) * 4.0, total)
    scale = 1.0 / total
    turn_real = (gain_real * lag_cos + gain_imag * lag_sin) * scale
    turn_imag = (gain_imag * lag_cos - gain_real * lag_sin) * scale
    cos, sin = turns(iota(shape, 0).astype(F32) * iota(shape, 1).astype(F32), n_group)
    shaped_real = turn_real * cos + turn_imag * sin
    shaped_imag = turn_imag * cos - turn_real * sin
    mid_op[...] = triple(dot_exact(
        stack2(cos, -sin, sin, cos), stack2(shaped_real, -shaped_imag, shaped_imag, shaped_real)
    ))

    arrived(0, got_a)
    pix[:blocks] = got_a[2 * blocks:3 * blocks].astype(jnp.int32)
    mark(blocks)
    look(blocks)
    phase, power = kick(blocks, got_a[:blocks], got_a[blocks:2 * blocks])
    deposit(blocks)
    result = diffract(me != total - 2)
    for a in range(n_active):
        send1[a * 2 * ROWS:a * 2 * ROWS + ROWS] = result[a * ROWS:(a + 1) * ROWS, :grid]
        send1[a * 2 * ROWS + ROWS:(a + 1) * 2 * ROWS] = result[a * ROWS:(a + 1) * ROWS, grid:]

    def to_active(i):
        a = (i + my_active) % n_active
        push(1, rows_of(send1, a, 2 * ROWS), rows_of(recv1, c, 2 * ROWS), 3 * (a // 2) + a % 2, g)
    repeat(n_active, to_active)

    target = got_a[3 * blocks:3 * blocks + 1, :blocks]
    square = (blocks, blocks)
    wide = jnp.broadcast_to(target, square)
    tall = jnp.sum(jnp.where(iota(square, 0) == iota(square, 1), wide, 0.0), axis=1, keepdims=True)
    same = jnp.logical_and(jnp.broadcast_to(tall, square) == wide, iota(square, 0) < iota(square, 1))
    rank = jnp.sum(jnp.where(same, 1.0, 0.0), axis=0, keepdims=True)
    payload = jnp.concatenate([phase, power, got_a[2 * blocks:3 * blocks] + 1.0], axis=1)
    shape = (n_cuts, blocks)
    goes = jnp.broadcast_to(target, shape) == iota(shape, 0).astype(F32)
    send_e[...] = jnp.zeros_like(send_e)
    for slot in range(2):
        pick = jnp.logical_and(goes, jnp.broadcast_to(rank, shape) == float(slot))
        moved = dot_exact(jnp.where(pick, 1.0, 0.0), payload)
        for part in range(3):
            send_e[pl.ds(slot * 3 + part, n_cuts, stride=8), :] = moved[:, part * width:(part + 1) * width]
    carry_cut = jnp.where(jnp.logical_and(g >= n_group - 3, g <= n_group - 2), 1, 0)

    def to_cut(i):
        k = (i + c) % n_cuts
        push(5, rows_of(send_e, k, 8), rows_of(recv_e, c, 8), (k + carry_cut) % n_cuts, ahead_group)

    @pl.when(active)
    def _():
        arrived(1, recv1)
        real = [recv1[pl.ds(j, n_cuts, stride=2 * ROWS), :] for j in range(ROWS)]
        imag = [recv1[pl.ds(ROWS + j, n_cuts, stride=2 * ROWS), :] for j in range(ROWS)]
        data = jnp.concatenate([jnp.concatenate(real, axis=1), jnp.concatenate(imag, axis=1)], axis=0)
        spec = apply_triple(cut_fwd[...], data)
        for j in range(ROWS):
            at = (j // HALF) * 2 * HALF + j % HALF
            send2[pl.ds(at, n_cuts, stride=2 * ROWS), :] = spec[:n_cuts, j * grid:(j + 1) * grid]
            send2[pl.ds(at + HALF, n_cuts, stride=2 * ROWS), :] = spec[n_cuts:, j * grid:(j + 1) * grid]

        def to_idle(i):
            push(2, rows_of(send2, n_group + i, 8), rows_of(recv2, g, 8), idle_cut, half_group * lane + i)
        def to_member(i):
            m = (i + g) % n_group
            push(2, rows_of(send2, m, 8), rows_of(recv2, g, 8), c, m)
        repeat(half_group, to_idle)
        repeat(n_group, to_member)
        repeat(n_cuts, to_cut)

    arrived(2, recv2)
    real = [recv2[pl.ds(j, n_group, stride=8), :] for j in range(HALF)]
    imag = [recv2[pl.ds(HALF + j, n_group, stride=8), :] for j in range(HALF)]
    data = jnp.concatenate([jnp.concatenate(real, axis=1), jnp.concatenate(imag, axis=1)], axis=0)
    shaped = apply_triple(mid_op[...], data)
    for j in range(HALF):
        send3[pl.ds(j, n_group, stride=8), :] = shaped[:n_group, j * grid:(j + 1) * grid]
        send3[pl.ds(HALF + j, n_group, stride=8), :] = shaped[n_group:, j * grid:(j + 1) * grid]

    def to_owner(i):
        m = (i + g) % n_group
        push(3, rows_of(send3, m, 8), rows_of(recv3, unit, 8), owner, m)
    repeat(n_group, to_owner)

    @pl.when(jnp.logical_not(active))
    def _():
        repeat(n_cuts, to_cut)

    @pl.when(active)
    def _():
        arrived(3, recv3)
        real, imag = [], []
        for j in range(ROWS):
            at = (j // HALF) * 2 * HALF + j % HALF
            real.append(recv3[pl.ds(at, n_cuts, stride=2 * ROWS), :])
            imag.append(recv3[pl.ds(at + HALF, n_cuts, stride=2 * ROWS), :])
        data = jnp.concatenate([jnp.concatenate(real, axis=1), jnp.concatenate(imag, axis=1)], axis=0)
        back = apply_triple(cut_inv[...], data)
        for j in range(ROWS):
            send4[pl.ds(j, n_cuts, stride=2 * ROWS), :] = back[:n_cuts, j * grid:(j + 1) * grid]
            send4[pl.ds(ROWS + j, n_cuts, stride=2 * ROWS), :] = back[n_cuts:, j * grid:(j + 1) * grid]

        def to_slice(i):
            k = (i + c) % n_cuts
            push(4, rows_of(send4, k, 2 * ROWS), rows_of(recv4, my_active, 2 * ROWS), k, g)
        repeat(n_cuts, to_slice)

    arrived(5, recv_e)
    def pieces(part):
        return jnp.concatenate(
            [recv_e[pl.ds(part, n_cuts, stride=8), :], recv_e[pl.ds(3 + part, n_cuts, stride=8), :]], axis=0
        )
    cells = pieces(2)
    slip_p[...] = cells
    remote(6, slip_p, got_p, before // n_group, before % n_group).start()
    pix[...] = (cells + 0.25).astype(jnp.int32) - 1
    mark(many)
    arrived(4, recv4)
    for a in range(n_active):
        field[a * ROWS:(a + 1) * ROWS] = recv4[a * 2 * ROWS:a * 2 * ROWS + ROWS]
        field[grid + a * ROWS:grid + (a + 1) * ROWS] = recv4[a * 2 * ROWS + ROWS:(a + 1) * 2 * ROWS]

    look(many)
    phase, power = kick(many, pieces(0), pieces(1))
    slip_b[:many] = phase
    slip_b[many:] = power
    remote(7, slip_b, got_b, before // n_group, before % n_group).start()
    deposit(many)
    set_field(diffract(me != 1))

    arrived(6, got_p)
    pix[...] = (got_p[...] + 0.25).astype(jnp.int32) - 1
    mark(many)
    look(many)
    arrived(7, got_b)
    kick(many, got_b[:many], got_b[many:])
    deposit(many)
    result = diffract(me != 0)
    out[0, 0] = result[:, :grid]
    out[0, 1] = result[:, grid:]

    sent(0, slip_a)
    sent(6, slip_p)
    sent(7, slip_b)
    sent(5, send_e)

    @pl.when(active)
    def _():
        sent(1, send1.at[pl.ds(0, (n_active - 1) * 2 * ROWS)])
        sent(2, send2.at[pl.ds(0, (units - 1) * 8)])
        sent(3, send3.at[pl.ds(0, (n_group - 1) * 8)])
        sent(4, send4.at[pl.ds(0, (n_cuts - 1) * 2 * ROWS)])

    @pl.when(jnp.logical_not(active))
    def _():
        sent(1, send1)
        sent(3, send3)


def on_device(n_cuts, n_group, radiation, phases, energy, pixels, destination, propagator, transmit):
    grid = radiation.shape[-1]
    blocks, width = phases.shape[1:]
    many = 2 * n_cuts
    chunk = 8 if many % 8 == 0 else many
    marks = (max(blocks, many) // chunk, grid, chunk * width)
    if blocks % 8 or many % 8:
        marks = (1, grid, many * width)
    n_active = grid // ROWS
    vmem = lambda shape, kind=F32: pltpu.VMEM(shape, kind)
    sizes = [n_active * 2 * ROWS, n_cuts * 2 * ROWS, n_cuts * 16, n_group * 8,
             n_group * 8, n_cuts * 16, n_cuts * 2 * ROWS, n_active * 2 * ROWS]
    scratch = [
        vmem((2 * grid, grid)),
        vmem((2 * grid, 2 * grid), BF16),
        vmem((2 * grid, 2 * grid), BF16),
        vmem((2 * n_cuts, 6 * n_cuts), BF16),
        vmem((2 * n_cuts, 6 * n_cuts), BF16),
        vmem((2 * n_group, 6 * n_group), BF16),
        vmem((3 * blocks + 8, width)),
        vmem((3 * blocks + 8, width)),
        vmem((many, width)),
        vmem((many, width)),
        vmem((2 * many, width)),
        vmem((2 * many, width)),
        vmem((many, width), jnp.int32),
        vmem(marks, BF16),
        vmem((2, many, width)),
        vmem((2, many, width)),
        vmem((2 * grid, grid)),
    ]
    scratch += [vmem((rows, grid)) for rows in sizes]
    scratch += [vmem((n_cuts * 8, width)), vmem((n_cuts * 8, width))]
    scratch += [pltpu.SemaphoreType.DMA((8,)), pltpu.SemaphoreType.DMA((8,))]
    return pl.pallas_call(
        functools.partial(kernel, n_cuts, n_group, grid, blocks, width),
        out_shape=jax.ShapeDtypeStruct(radiation.shape, F32),
        in_specs=[pl.BlockSpec(memory_space=pltpu.VMEM)] * 7,
        out_specs=pl.BlockSpec(memory_space=pltpu.VMEM),
        scratch_shapes=scratch,
        compiler_params=pltpu.CompilerParams(collective_id=0, has_side_effects=True),
    )(radiation, phases, energy, pixels, destination, propagator, transmit)


def solution(mesh):
    sizes = dict(mesh.shape)
    return jax.shard_map(
        functools.partial(on_device, sizes["cuts"], sizes["group"]),
        mesh=mesh,
        in_specs=(
            P(("cuts", "group"), None, None, None),
            P(("cuts", "group"), None, None),
            P(("cuts", "group"), None, None),
            P(("cuts", "group"), None, None),
            P(("cuts", "group"), None),
            P(),
            P(),
        ),
        out_specs=P(("cuts", "group"), None, None, None),
        check_vma=False,
    )
```

profile of v0, /device:TPU:1, one launch (start us, length us, event | category | flops | bytes accessed | tf_op | source)
XLA Modules:
  0.0 72.2 jit_solution(8813448257585604139)
XLA Ops:
  0.0 70.7 %shard_map.73 = f32[1,2,128,128]{3,2,1,0:T(8,128)} custom-call(f32[1,2,128,128]{3,2,1,0:T(8,128)} %radiation.1, f32[1,16,128]{2,1,0:T(8,128)} %phases.1, f32[1,16,128]{2,1,0:T(8,128)} %energy.1, s32[1,16,128]{2,1,0:T(8,128)} %pixels.1, s32[1,16]{1,0:T(1,128)} %destination.1, f32[2,128,128]{2,1,0:T(8,128)} %propagator.1, f32[2,768]{1,0:T(2,128)} %transmit.1), custom_call_target="tpu_custom_call" | custom-call | tf_op jit(solution)/shard_map/pallas_call | solution.py:457
  70.7 1.6 %copy.9 = f32[1,2,128,128]{3,2,1,0:T(8,128)} copy(f32[1,2,128,128]{3,2,1,0:T(8,128)} %shard_map.73) | data formatting | bytes 262144
where the time goes:
time: 72.8 us; the launch traced here: 72.2 us
  Pallas kernels  70.7 us (97%)
  local copies, waits for them, and re-layouts  1.57 us (2%)
    pallas_call x1, Pallas kernels, on_device(): pl.pallas_call(functools.partial(kernel, n_cuts, n_group, grid, blocks, w...  70.7 us
    unnamed x1, local copies, waits for them, and re-layouts  1.57 us

commit v1 on v0

v1 whole, which is shorter than its diff:
```python
import contextlib
import functools
import math

import jax
import jax.numpy as jnp
from jax import lax
from jax.experimental import pallas as pl
from jax.experimental.pallas import tpu as pltpu
from jax.sharding import PartitionSpec as P

KICK_RATE = 0.5
PHASE_RATE = 1.0
EMIT_RATE = 0.5
F32 = jnp.float32
BF16 = jnp.bfloat16
MESH = pl.DeviceIdType.MESH
ROWS = 8
HALF = 4


def tag(name):
    return contextlib.nullcontext()


def iota(shape, dim):
    return lax.broadcasted_iota(jnp.int32, shape, dim)


def split(x):
    high = x.astype(BF16)
    return high, (x - high.astype(F32)).astype(BF16)


def dot(a, b):
    return jnp.dot(a, b, preferred_element_type=F32)


def dot_nt(a, b):
    return lax.dot_general(a, b, (((1,), (1,)), ((), ())), preferred_element_type=F32)


def dot_exact(a, b):
    return jnp.dot(a, b, precision=lax.Precision.HIGHEST, preferred_element_type=F32)


def turns(product, total):
    whole = jnp.floor((product + 0.5) * (1.0 / total))
    angle = (product - whole * total) * (2.0 * math.pi / total)
    return jnp.cos(angle), jnp.sin(angle)


def stack2(a, b, c, d):
    return jnp.concatenate(
        [jnp.concatenate([a, b], axis=1), jnp.concatenate([c, d], axis=1)], axis=0
    )


def triple(matrix):
    high, low = split(matrix)
    return jnp.concatenate([high, high, low], axis=1)


def apply_triple(packed, data):
    high, low = split(data)
    return dot(packed, jnp.concatenate([high, low, high], axis=0))


def kernel(
    n_cuts, n_group, grid, blocks, width,
    radiation, phases, energy, pixels, destination, propagator, transmit,
    out,
    phase_in, power_in, pixel_in, target_in, prop_in, gain_in, result_out,
    field, prop_hi, prop_lo, cut_fwd, cut_inv, mid_op,
    slip_a, got_a, slip_e, slip_p, got_p, slip_b, got_b,
    hot_now, hot_next, row_now, row_next, read, weight, source,
    send1, recv1, send2, recv2, send3, recv3, send4, recv4, send_e, recv_e,
    load_sems, send_sems, recv_sems,
):
    c = lax.axis_index("cuts")
    g = lax.axis_index("group")
    total = n_cuts * n_group
    me = c * n_group + g
    n_active = grid // ROWS
    lane = c % 3
    active = lane != 1
    idle = jnp.logical_not(active)
    side = lane // 2
    idle_cut = c - lane + 1
    half_group = n_group // 2
    my_active = 2 * (c // 3) + side
    owner = jnp.where(active, c, c - 1 + 2 * (g // half_group))
    unit = jnp.where(active, g, n_group + g % half_group)
    many = 2 * n_cuts

    def device(offset):
        other = (me + total + offset) % total
        return other // n_group, other % n_group

    def repeat(count, body):
        def step(i, carry):
            body(i)
            return carry
        lax.fori_loop(0, count, step, 0)

    loads = [
        pltpu.make_async_copy(src, dst, load_sems.at[i])
        for i, (src, dst) in enumerate([
            (pixels.at[0], pixel_in), (radiation.at[0, 0], field.at[pl.ds(0, grid)]),
            (radiation.at[0, 1], field.at[pl.ds(grid, grid)]), (phases.at[0], phase_in),
            (energy.at[0], power_in), (destination, target_in), (propagator, prop_in), (transmit, gain_in),
        ])
    ]
    for load in loads:
        load.start()
    barrier = pltpu.get_barrier_semaphore()

    def hello(cc, gg):
        pl.semaphore_signal(barrier, inc=1, device_id=(cc, gg), device_id_type=MESH)

    for offset in (-1, 1, -3, 3):
        hello(*device(offset))
    repeat(n_cuts - 1, lambda i: hello((c + 1 + i) % n_cuts, g))

    @pl.when(active)
    def _():
        repeat(n_group - 1, lambda i: hello(c, (g + 1 + i) % n_group))
        repeat(half_group, lambda i: hello(idle_cut, half_group * side + i))

    @pl.when(idle)
    def _():
        repeat(n_group, lambda i: hello(owner, (g + i) % n_group))

    def meet():
        greeted = 4 + n_cuts - 1

        @pl.when(active)
        def _():
            pl.semaphore_wait(barrier, greeted + n_group - 1 + half_group)

        @pl.when(idle)
        def _():
            pl.semaphore_wait(barrier, greeted + n_group)

    def remote(stage, src, dst, cc, gg):
        return pltpu.make_async_remote_copy(
            src_ref=src, dst_ref=dst, send_sem=send_sems.at[stage], recv_sem=recv_sems.at[stage],
            device_id=(cc, gg), device_id_type=MESH,
        )

    def push(stage, src, dst, cc, gg):
        mine = jnp.logical_and(cc == c, gg == g)

        @pl.when(mine)
        def _():
            pltpu.make_async_copy(src, dst, recv_sems.at[stage]).start()

        @pl.when(jnp.logical_not(mine))
        def _():
            remote(stage, src, dst, cc, gg).start()

    def arrived(stage, ref):
        with tag("wait%d" % stage):
            remote(stage, ref, ref, c, g).wait_recv()

    def sent(stage, ref):
        remote(stage, ref, ref, c, g).wait_send()

    def tile(ref, index):
        return ref.at[pl.ds(pl.multiple_of(index * 8, 8), 8)]

    shift = grid.bit_length()
    pairs = grid // 2
    places = 2 * grid

    def chunk_of(count):
        return 8 if count % 8 == 0 else count

    def mark(count, cells, hot, rows):
        chunk = chunk_of(count)
        for i in range(count // chunk):
            part = cells[i * chunk:(i + 1) * chunk]
            rows[i * chunk:(i + 1) * chunk] = lax.shift_right_arithmetic(part, shift)
            place = part & (places - 1)
            for b in range(chunk):
                match = iota((places, width), 0) == jnp.broadcast_to(place[b:b + 1], (places, width))
                hot[i, :, b * width:(b + 1) * width] = jnp.where(match, 1.0, 0.0).astype(BF16)

    def look(count, hot, rows):
        chunk = chunk_of(count)
        low = jnp.concatenate([field[pl.ds(0, grid, stride=2), :], field[pl.ds(1, grid, stride=2), :]], axis=1).astype(BF16)
        def body(i):
            first = pl.multiple_of(i * chunk, chunk)
            at = rows[pl.ds(first, chunk), :]
            real, imag = [], []
            for two in range(chunk // 2):
                picked = dot(low, hot[i, :, two * 2 * width:(two + 1) * 2 * width])
                for b in range(2):
                    match = iota((pairs, width), 0) == jnp.broadcast_to(at[2 * two + b:2 * two + b + 1], (pairs, width))
                    part = picked[:, b * width:(b + 1) * width]
                    real.append(jnp.sum(jnp.where(match, part[:pairs], 0.0), axis=0, keepdims=True))
                    imag.append(jnp.sum(jnp.where(match, part[pairs:], 0.0), axis=0, keepdims=True))
            read[0, pl.ds(first, chunk), :] = jnp.concatenate(real, axis=0)
            read[1, pl.ds(first, chunk), :] = jnp.concatenate(imag, axis=0)
        repeat(count // chunk, body)

    def kick(count, phase, power, cos, sin):
        power = power - KICK_RATE * (read[0, :count] * cos - read[1, :count] * sin)
        phase = phase + PHASE_RATE * power
        weight[0, :count] = jnp.cos(phase)
        weight[1, :count] = -jnp.sin(phase)
        return phase, power

    def deposit(count, hot, rows):
        chunk = chunk_of(count)
        source[...] = jnp.zeros_like(source)
        def body(i):
            first = pl.multiple_of(i * chunk, chunk)
            at = rows[pl.ds(first, chunk), :]
            real = weight[0, pl.ds(first, chunk), :]
            imag = weight[1, pl.ds(first, chunk), :]
            tops, bottoms = [], []
            shape = (pairs, width)
            for b in range(chunk):
                match = iota(shape, 0) == jnp.broadcast_to(at[b:b + 1], shape)
                tops.append(jnp.where(match, jnp.broadcast_to(real[b:b + 1], shape), 0.0).astype(BF16))
                bottoms.append(jnp.where(match, jnp.broadcast_to(imag[b:b + 1], shape), 0.0).astype(BF16))
            spread = jnp.concatenate([jnp.concatenate(tops, axis=1), jnp.concatenate(bottoms, axis=1)], axis=0)
            source[...] += dot_nt(spread, hot[i])
        repeat(count // chunk, body)

    def emit():
        field[pl.ds(0, grid, stride=2), :] = field[pl.ds(0, grid, stride=2), :] + EMIT_RATE * source[:, :grid]
        field[pl.ds(1, grid, stride=2), :] = field[pl.ds(1, grid, stride=2), :] + EMIT_RATE * source[:, grid:]

    def diffract(keep):
        emit()
        high, low = split(field[...])
        both = dot(prop_hi[...], jnp.concatenate([high, low], axis=1))
        left = both[:, :grid] + both[:, grid:] + dot(prop_lo[...], high)
        left = jnp.concatenate([left[:grid], left[grid:]], axis=1)
        high, low = split(left)
        result = dot_nt(high, prop_hi[...]) + dot_nt(low, prop_hi[...]) + dot_nt(high, prop_lo[...])
        return jnp.where(keep, result, 0.0)

    def set_field(result):
        field[:grid] = result[:, :grid]
        field[grid:] = result[:, grid:]

    loads[0].wait()
    mark(blocks, pixel_in[...], hot_now, row_now)
    for load in loads[1:]:
        load.wait()
    look(blocks, hot_now, row_now)
    phase = phase_in[...]
    phase, power = kick(blocks, phase, power_in[...], jnp.cos(phase), jnp.sin(phase))
    slip_a[:blocks] = phase
    slip_a[blocks:2 * blocks] = power
    slip_a[2 * blocks:3 * blocks] = pixel_in[...].astype(F32)
    slip_a[3 * blocks:] = jnp.zeros_like(slip_a[3 * blocks:])
    slip_a[3 * blocks:3 * blocks + 1, :blocks] = target_in[...].astype(F32)
    with tag("meet"):
        meet()
    remote(0, slip_a, got_a, *device(-1)).start()
    prop = stack2(prop_in[0], -prop_in[1], prop_in[1], prop_in[0])
    high, low = split(prop)
    prop_hi[...] = high
    prop_lo[...] = low
    deposit(blocks, hot_now, row_now)
    set_field(diffract(me != total - 1))

    arrived(0, got_a)
    mark(blocks, got_a[2 * blocks:3 * blocks].astype(jnp.int32), hot_now, row_now)
    look(blocks, hot_now, row_now)
    phase = got_a[:blocks]
    phase, power = kick(blocks, phase, got_a[blocks:2 * blocks], jnp.cos(phase), jnp.sin(phase))
    deposit(blocks, hot_now, row_now)
    result = diffract(me != total - 2)
    for a in range(n_active):
        for h in range(2):
            at = a * ROWS + h * HALF
            send1[h, a * 8:a * 8 + HALF] = result[at:at + HALF, :grid]
            send1[h, a * 8 + HALF:(a + 1) * 8] = result[at:at + HALF, grid:]

    for h in range(2):
        def to_active(i):
            a = (i + my_active) % n_active
            push(1 + h, tile(send1.at[h], a), tile(recv1.at[h], c), 3 * (a // 2) + 2 * (a % 2), g)
        repeat(n_active, to_active)

    target = got_a[3 * blocks:3 * blocks + 1, :blocks]
    square = (blocks, blocks)
    wide = jnp.broadcast_to(target, square)
    tall = jnp.sum(jnp.where(iota(square, 0) == iota(square, 1), wide, 0.0), axis=1, keepdims=True)
    same = jnp.logical_and(jnp.broadcast_to(tall, square) == wide, iota(square, 0) < iota(square, 1))
    rank = jnp.sum(jnp.where(same, 1.0, 0.0), axis=0, keepdims=True)
    payload = jnp.concatenate([phase, power, got_a[2 * blocks:3 * blocks] + 1.0], axis=1)
    shape = (n_cuts, blocks)
    goes = jnp.broadcast_to(target, shape) == iota(shape, 0).astype(F32)
    send_e[...] = jnp.zeros_like(send_e)
    for slot in range(2):
        pick = jnp.logical_and(goes, jnp.broadcast_to(rank, shape) == float(slot))
        moved = dot_exact(jnp.where(pick, 1.0, 0.0), payload)
        for part in range(3):
            send_e[pl.ds(slot * 3 + part, n_cuts, stride=8), :] = moved[:, part * width:(part + 1) * width]
    borrow = jnp.where(g == n_group - 1, n_cuts - 1, n_cuts)

    def to_cut(i):
        k = (i + c) % n_cuts
        push(9, tile(send_e, k), tile(recv_e, c), (k + borrow) % n_cuts, g)

    shape = (n_cuts, n_cuts)
    g_real = g.astype(F32)
    cos, sin = turns((iota(shape, 1).astype(F32) * n_group + g_real) * iota(shape, 0).astype(F32), total)
    cut_fwd[...] = triple(stack2(cos, sin, -sin, cos))
    cos, sin = turns((iota(shape, 0).astype(F32) * n_group + g_real) * iota(shape, 1).astype(F32), total)
    cut_inv[...] = triple(stack2(cos, -sin, sin, cos))
    first_freq = unit // 2
    shape = (n_group, total)
    chosen = iota(shape, 1) == first_freq + n_cuts * iota(shape, 0)
    gain_real = jnp.sum(jnp.where(chosen, jnp.broadcast_to(gain_in[0:1], shape), 0.0), axis=1, keepdims=True)
    gain_imag = jnp.sum(jnp.where(chosen, jnp.broadcast_to(gain_in[1:2], shape), 0.0), axis=1, keepdims=True)
    shape = (n_group, n_group)
    lag_cos, lag_sin = turns((first_freq.astype(F32) + n_cuts * iota(shape, 0).astype(F32)) * 4.0, total)
    scale = 1.0 / total
    turn_real = (gain_real * lag_cos + gain_imag * lag_sin) * scale
    turn_imag = (gain_imag * lag_cos - gain_real * lag_sin) * scale
    cos, sin = turns(iota(shape, 0).astype(F32) * iota(shape, 1).astype(F32), n_group)
    shaped_real = turn_real * cos + turn_imag * sin
    shaped_imag = turn_imag * cos - turn_real * sin
    mid_op[...] = triple(dot_exact(
        stack2(cos, -sin, sin, cos), stack2(shaped_real, -shaped_imag, shaped_imag, shaped_real)
    ))

    def apply(operator, count, source_ref, target_ref):
        real = [source_ref[pl.ds(j, count, stride=8), :] for j in range(HALF)]
        imag = [source_ref[pl.ds(HALF + j, count, stride=8), :] for j in range(HALF)]
        data = jnp.concatenate([jnp.concatenate(real, axis=1), jnp.concatenate(imag, axis=1)], axis=0)
        done = apply_triple(operator[...], data)
        for j in range(HALF):
            target_ref[pl.ds(j, count, stride=8), :] = done[:count, j * grid:(j + 1) * grid]
            target_ref[pl.ds(HALF + j, count, stride=8), :] = done[count:, j * grid:(j + 1) * grid]

    @pl.when(active)
    def _():
        for h in range(2):
            arrived(1 + h, recv1.at[h])
            with tag("fwd%d" % h):
                apply(cut_fwd, n_cuts, recv1.at[h], send2.at[h])
            def to_unit(i):
                freq = (i + (3 * g) // 4) % n_cuts
                u = 2 * freq + h
                own = u < n_group
                push(
                    3, tile(send2.at[h], freq), tile(recv2, g),
                    jnp.where(own, c, idle_cut), jnp.where(own, u, half_group * side + u - n_group),
                )
            with tag("send2%d" % h):
                repeat(n_cuts, to_unit)
        with tag("sende"):
            repeat(n_cuts, to_cut)

    arrived(3, recv2)
    with tag("mid"):
        apply(mid_op, n_group, recv2, send3)

    for h in range(2):
        @pl.when(unit % 2 == h)
        def _():
            def to_owner(i):
                m = (i + g) % n_group
                push(4 + h, tile(send3, m), tile(recv3.at[h], unit // 2), owner, m)
            with tag("send3"):
                repeat(n_group, to_owner)

    @pl.when(idle)
    def _():
        with tag("sende"):
            repeat(n_cuts, to_cut)

    @pl.when(active)
    def _():
        for h in range(2):
            arrived(4 + h, recv3.at[h])
            with tag("inv%d" % h):
                apply(cut_inv, n_cuts, recv3.at[h], send4.at[h])
            def to_slice(i):
                k = (i + c) % n_cuts
                push(6 + h, tile(send4.at[h], k), tile(recv4.at[h], my_active), k, g)
            with tag("send4%d" % h):
                repeat(n_cuts, to_slice)

    arrived(9, recv_e)
    remote(10, recv_e, slip_e, *device(3)).start()
    arrived(10, slip_e)

    def pieces(part):
        return jnp.concatenate(
            [slip_e[pl.ds(part, n_cuts, stride=8), :], slip_e[pl.ds(3 + part, n_cuts, stride=8), :]], axis=0
        )

    def cells_of(value):
        return (value + 0.25).astype(jnp.int32) - 1

    cells = pieces(2)
    slip_p[...] = cells
    remote(11, slip_p, got_p, *device(-1)).start()
    with tag("mark3"):
        mark(many, cells_of(cells), hot_now, row_now)
    phase = pieces(0)
    cos, sin = jnp.cos(phase), jnp.sin(phase)
    arrived(11, got_p)
    with tag("mark4"):
        mark(many, cells_of(got_p[...]), hot_next, row_next)
    for h in range(2):
        arrived(6 + h, recv4.at[h])
        for a in range(n_active):
            at = a * ROWS + h * HALF
            field[at:at + HALF] = recv4[h, a * 8:a * 8 + HALF]
            field[grid + at:grid + at + HALF] = recv4[h, a * 8 + HALF:(a + 1) * 8]

    with tag("look3"):
        look(many, hot_now, row_now)
    with tag("kick3"):
        phase, power = kick(many, phase, pieces(1), cos, sin)
        slip_b[:many] = phase
        slip_b[many:] = power
    remote(12, slip_b, got_b, *device(-1)).start()
    with tag("deposit3"):
        deposit(many, hot_now, row_now)
    with tag("diffract3"):
        set_field(diffract(me != 1))

    with tag("look4"):
        look(many, hot_next, row_next)
    arrived(12, got_b)
    with tag("kick4"):
        phase = got_b[:many]
        kick(many, phase, got_b[many:], jnp.cos(phase), jnp.sin(phase))
    with tag("deposit4"):
        deposit(many, hot_next, row_next)
    with tag("diffract4"):
        result = diffract(me != 0)
        result_out[0] = result[:, :grid]
        result_out[1] = result[:, grid:]
    store = pltpu.make_async_copy(result_out, out.at[0], load_sems.at[0])
    store.start()

    sent(0, slip_a)
    sent(9, send_e.at[pl.ds(0, (n_cuts - 1) * 8)])
    sent(10, recv_e)
    sent(11, slip_p)
    sent(12, slip_b)

    @pl.when(active)
    def _():
        for h in range(2):
            sent(1 + h, send1.at[h, pl.ds(0, (n_active - 1) * 8)])
            sent(6 + h, send4.at[h, pl.ds(0, (n_cuts - 1) * 8)])
        for h in range(2):
            @pl.when(unit % 2 == h)
            def _():
                sent(4 + h, send3.at[pl.ds(0, (n_group - 1) * 8)])
        sent(3, send2.at[0])
        sent(3, send2.at[1, pl.ds(0, (n_cuts - 1) * 8)])

    @pl.when(idle)
    def _():
        for h in range(2):
            sent(1 + h, send1.at[h])
            @pl.when(unit % 2 == h)
            def _():
                sent(4 + h, send3)
    store.wait()


def on_device(n_cuts, n_group, radiation, phases, energy, pixels, destination, propagator, transmit):
    grid = radiation.shape[-1]
    blocks, width = phases.shape[1:]
    many = 2 * n_cuts
    chunk = 8 if many % 8 == 0 else many
    marks = (many // chunk, 2 * grid, chunk * width)
    n_active = grid // ROWS
    vmem = lambda shape, kind=F32: pltpu.VMEM(shape, kind)
    scratch = [
        vmem((blocks, width)), vmem((blocks, width)), vmem((blocks, width), jnp.int32),
        vmem(destination.shape, jnp.int32), vmem(propagator.shape), vmem(transmit.shape), vmem(radiation.shape[1:]),
        vmem((2 * grid, grid)),
        vmem((2 * grid, 2 * grid), BF16), vmem((2 * grid, 2 * grid), BF16),
        vmem((2 * n_cuts, 6 * n_cuts), BF16), vmem((2 * n_cuts, 6 * n_cuts), BF16),
        vmem((2 * n_group, 6 * n_group), BF16),
        vmem((3 * blocks + 8, width)), vmem((3 * blocks + 8, width)),
        vmem((n_cuts * 8, width)),
        vmem((many, width)), vmem((many, width)),
        vmem((2 * many, width)), vmem((2 * many, width)),
        vmem(marks, BF16), vmem(marks, BF16),
        vmem((many, width), jnp.int32), vmem((many, width), jnp.int32),
        vmem((2, many, width)), vmem((2, many, width)),
        vmem((grid, 2 * grid)),
        vmem((2, n_active * 8, grid)), vmem((2, n_cuts * 8, grid)),
        vmem((2, n_cuts * 8, grid)), vmem((n_group * 8, grid)),
        vmem((n_group * 8, grid)), vmem((2, n_cuts * 8, grid)),
        vmem((2, n_cuts * 8, grid)), vmem((2, n_active * 8, grid)),
        vmem((n_cuts * 8, width)), vmem((n_cuts * 8, width)),
        pltpu.SemaphoreType.DMA((8,)), pltpu.SemaphoreType.DMA((13,)), pltpu.SemaphoreType.DMA((13,)),
    ]
    return pl.pallas_call(
        functools.partial(kernel, n_cuts, n_group, grid, blocks, width),
        out_shape=jax.ShapeDtypeStruct(radiation.shape, F32),
        in_specs=[pl.BlockSpec(memory_space=pl.ANY)] * 7,
        out_specs=pl.BlockSpec(memory_space=pl.ANY),
        scratch_shapes=scratch,
        compiler_params=pltpu.CompilerParams(collective_id=0, has_side_effects=True),
    )(radiation, phases, energy, pixels, destination, propagator, transmit)


def solution(mesh):
    sizes = dict(mesh.shape)
    return jax.shard_map(
        functools.partial(on_device, sizes["cuts"], sizes["group"]),
        mesh=mesh,
        in_specs=(
            P(("cuts", "group"), None, None, None),
            P(("cuts", "group"), None, None),
            P(("cuts", "group"), None, None),
            P(("cuts", "group"), None, None),
            P(("cuts", "group"), None),
            P(),
            P(),
        ),
        out_specs=P(("cuts", "group"), None, None, None),
        check_vma=False,
    )
```

time: 72.8 us -> 72.8 us (level)
  no operation moved by 1% of the time
where the time goes in v1:
time: 72.8 us; the launch traced here: 72.7 us
  Pallas kernels  71.1 us (98%)
  local copies, waits for them, and re-layouts  1.57 us (2%)
    pallas_call x1, Pallas kernels, on_device(): pl.pallas_call(functools.partial(kernel, n_cuts, n_group, grid, blocks, w...  71.1 us
    unnamed x1, local copies, waits for them, and re-layouts  1.57 us

profile of v1, /device:TPU:1, one launch (start us, length us, event | category | flops | bytes accessed | tf_op | source)
XLA Modules:
  0.0 72.7 jit_solution(7778611603852719977)
XLA Ops:
  0.0 71.1 %shard_map.73 = f32[1,2,128,128]{3,2,1,0:T(8,128)} custom-call(f32[1,2,128,128]{3,2,1,0:T(8,128)} %radiation.1, f32[1,16,128]{2,1,0:T(8,128)} %phases.1, f32[1,16,128]{2,1,0:T(8,128)} %energy.1, s32[1,16,128]{2,1,0:T(8,128)} %pixels.1, s32[1,16]{1,0:T(1,128)} %destination.1, f32[2,128,128]{2,1,0:T(8,128)} %propagator.1, f32[2,768]{1,0:T(2,128)} %transmit.1), custom_call_target="tpu_custom_call" | custom-call | tf_op jit(solution)/shard_map/pallas_call | solution.py:507
  71.1 1.6 %copy.9 = f32[1,2,128,128]{3,2,1,0:T(8,128)} copy(f32[1,2,128,128]{3,2,1,0:T(8,128)} %shard_map.73) | data formatting | bytes 262144

commit v2 on v1

--- a/solution.py
+++ b/solution.py
@@ -72,8 +72,8 @@
     out,
     phase_in, power_in, pixel_in, target_in, prop_in, gain_in, result_out,
     field, prop_hi, prop_lo, cut_fwd, cut_inv, mid_op,
-    slip_a, got_a, slip_e, slip_p, got_p, slip_b, got_b,
-    hot_now, hot_next, row_now, row_next, read, weight, source,
+    slip_a, got_a, slip_p, got_p, slip_b, got_b,
+    hot_now, hot_next, turned_now, turned_next, row_now, row_next, read, weight, source,
     send1, recv1, send2, recv2, send3, recv3, send4, recv4, send_e, recv_e,
     load_sems, send_sems, recv_sems,
 ):
@@ -82,26 +82,30 @@
     total = n_cuts * n_group
     me = c * n_group + g
     n_active = grid // ROWS
-    lane = c % 3
+    third = c // 3
+    lane = c - 3 * third
     active = lane != 1
     idle = jnp.logical_not(active)
     side = lane // 2
     idle_cut = c - lane + 1
     half_group = n_group // 2
-    my_active = 2 * (c // 3) + side
+    my_active = 2 * third + side
     owner = jnp.where(active, c, c - 1 + 2 * (g // half_group))
     unit = jnp.where(active, g, n_group + g % half_group)
     many = 2 * n_cuts
 
+    def wrap(value, size):
+        return jnp.where(value >= size, value - size, value)
+
     def device(offset):
-        other = (me + total + offset) % total
+        other = wrap(me + (offset + total if offset < 0 else offset), total)
         return other // n_group, other % n_group
 
     def repeat(count, body):
         def step(i, carry):
             body(i)
             return carry
-        lax.fori_loop(0, count, step, 0)
+        lax.fori_loop(0, count, step, 0, unroll=math.gcd(count, 4))
 
     loads = [
         pltpu.make_async_copy(src, dst, load_sems.at[i])
@@ -118,21 +122,29 @@
     def hello(cc, gg):
         pl.semaphore_signal(barrier, inc=1, device_id=(cc, gg), device_id_type=MESH)
 
-    for offset in (-1, 1, -3, 3):
-        hello(*device(offset))
-    repeat(n_cuts - 1, lambda i: hello((c + 1 + i) % n_cuts, g))
+    ahead_group = wrap(g + 3, n_group)
+    behind_group = wrap(g + n_group - 3, n_group)
+    ring = max(1, n_cuts // 2)
+    for j in sorted(range(n_cuts), key=lambda j: -min(j % ring, ring - j % ring)):
+        cut = wrap(c + j, n_cuts)
+        hello(cut, ahead_group)
+        hello(cut, behind_group)
+        if j:
+            hello(cut, g)
+    hello(*device(-1))
+    hello(*device(1))
 
     @pl.when(active)
     def _():
-        repeat(n_group - 1, lambda i: hello(c, (g + 1 + i) % n_group))
+        repeat(n_group - 1, lambda i: hello(c, wrap(g + 1 + i, n_group)))
         repeat(half_group, lambda i: hello(idle_cut, half_group * side + i))
 
     @pl.when(idle)
     def _():
-        repeat(n_group, lambda i: hello(owner, (g + i) % n_group))
+        repeat(n_group, lambda i: hello(owner, wrap(g + i, n_group)))
 
     def meet():
-        greeted = 4 + n_cuts - 1
+        greeted = 2 + n_cuts - 1 + 2 * n_cuts
 
         @pl.when(active)
         def _():
@@ -173,36 +185,32 @@
     pairs = grid // 2
     places = 2 * grid
 
-    def chunk_of(count):
-        return 8 if count % 8 == 0 else count
-
-    def mark(count, cells, hot, rows):
-        chunk = chunk_of(count)
-        for i in range(count // chunk):
-            part = cells[i * chunk:(i + 1) * chunk]
-            rows[i * chunk:(i + 1) * chunk] = lax.shift_right_arithmetic(part, shift)
-            place = part & (places - 1)
-            for b in range(chunk):
-                match = iota((places, width), 0) == jnp.broadcast_to(place[b:b + 1], (places, width))
-                hot[i, :, b * width:(b + 1) * width] = jnp.where(match, 1.0, 0.0).astype(BF16)
+    def mark(count, cells, hot, rows, turned=None):
+        rows[:count] = lax.shift_right_arithmetic(cells, shift)
+        place = cells & (places - 1)
+        for b in range(count):
+            match = iota((places, width), 0) == jnp.broadcast_to(place[b:b + 1], (places, width))
+            hot[:, b * width:(b + 1) * width] = jnp.where(match, 1.0, 0.0).astype(BF16)
+        if turned is not None:
+            columns = jnp.transpose(place.astype(F32))
+            spot = iota((width, places), 1).astype(F32)
+            for b in range(count):
+                match = spot == jnp.broadcast_to(columns[:, b:b + 1], (width, places))
+                turned[b * width:(b + 1) * width] = jnp.where(match, 1.0, 0.0).astype(BF16)
 
     def look(count, hot, rows):
-        chunk = chunk_of(count)
         low = jnp.concatenate([field[pl.ds(0, grid, stride=2), :], field[pl.ds(1, grid, stride=2), :]], axis=1).astype(BF16)
-        def body(i):
-            first = pl.multiple_of(i * chunk, chunk)
-            at = rows[pl.ds(first, chunk), :]
-            real, imag = [], []
-            for two in range(chunk // 2):
-                picked = dot(low, hot[i, :, two * 2 * width:(two + 1) * 2 * width])
-                for b in range(2):
-                    match = iota((pairs, width), 0) == jnp.broadcast_to(at[2 * two + b:2 * two + b + 1], (pairs, width))
-                    part = picked[:, b * width:(b + 1) * width]
-                    real.append(jnp.sum(jnp.where(match, part[:pairs], 0.0), axis=0, keepdims=True))
-                    imag.append(jnp.sum(jnp.where(match, part[pairs:], 0.0), axis=0, keepdims=True))
-            read[0, pl.ds(first, chunk), :] = jnp.concatenate(real, axis=0)
-            read[1, pl.ds(first, chunk), :] = jnp.concatenate(imag, axis=0)
-        repeat(count // chunk, body)
+        real, imag = [], []
+        for two in range(count // 2):
+            picked = dot(low, hot[:, two * 2 * width:(two + 1) * 2 * width])
+            for b in range(2):
+                at = rows[2 * two + b:2 * two + b + 1]
+                match = iota((pairs, width), 0) == jnp.broadcast_to(at, (pairs, width))
+                part = picked[:, b * width:(b + 1) * width]
+                real.append(jnp.sum(jnp.where(match, part[:pairs], 0.0), axis=0, keepdims=True))
+                imag.append(jnp.sum(jnp.where(match, part[pairs:], 0.0), axis=0, keepdims=True))
+        read[0, :count] = jnp.concatenate(real, axis=0)
+        read[1, :count] = jnp.concatenate(imag, axis=0)
 
     def kick(count, phase, power, cos, sin):
         power = power - KICK_RATE * (read[0, :count] * cos - read[1, :count] * sin)
@@ -211,23 +219,23 @@
         weight[1, :count] = -jnp.sin(phase)
         return phase, power
 
-    def deposit(count, hot, rows):
-        chunk = chunk_of(count)
-        source[...] = jnp.zeros_like(source)
-        def body(i):
-            first = pl.multiple_of(i * chunk, chunk)
-            at = rows[pl.ds(first, chunk), :]
-            real = weight[0, pl.ds(first, chunk), :]
-            imag = weight[1, pl.ds(first, chunk), :]
+    def deposit(count, hot, rows, turned=None):
+        chunk = 8 if count % 8 == 0 else count
+        shape = (pairs, width)
+        gathered = jnp.zeros((grid, places), F32)
+        for first in range(0, count, chunk):
             tops, bottoms = [], []
-            shape = (pairs, width)
-            for b in range(chunk):
-                match = iota(shape, 0) == jnp.broadcast_to(at[b:b + 1], shape)
-                tops.append(jnp.where(match, jnp.broadcast_to(real[b:b + 1], shape), 0.0).astype(BF16))
-                bottoms.append(jnp.where(match, jnp.broadcast_to(imag[b:b + 1], shape), 0.0).astype(BF16))
+            for b in range(first, first + chunk):
+                match = iota(shape, 0) == jnp.broadcast_to(rows[b:b + 1], shape)
+                tops.append(jnp.where(match, jnp.broadcast_to(weight[0, b:b + 1], shape), 0.0).astype(BF16))
+                bottoms.append(jnp.where(match, jnp.broadcast_to(weight[1, b:b + 1], shape), 0.0).astype(BF16))
             spread = jnp.concatenate([jnp.concatenate(tops, axis=1), jnp.concatenate(bottoms, axis=1)], axis=0)
-            source[...] += dot_nt(spread, hot[i])
-        repeat(count // chunk, body)
+            span = slice(first * width, (first + chunk) * width)
+            if turned is None:
+                gathered = gathered + dot_nt(spread, hot[:, span])
+            else:
+                gathered = gathered + dot(spread, turned[span])
+        source[...] = gathered
 
     def emit():
         field[pl.ds(0, grid, stride=2), :] = field[pl.ds(0, grid, stride=2), :] + EMIT_RATE * source[:, :grid]
@@ -284,8 +292,8 @@
 
     for h in range(2):
         def to_active(i):
-            a = (i + my_active) % n_active
-            push(1 + h, tile(send1.at[h], a), tile(recv1.at[h], c), 3 * (a // 2) + 2 * (a % 2), g)
+            a = wrap(i + my_active, n_active)
+            push(1 + h, tile(send1.at[h], a), tile(recv1.at[h], c), 3 * (a >> 1) + 2 * (a & 1), g)
         repeat(n_active, to_active)
 
     target = got_a[3 * blocks:3 * blocks + 1, :blocks]
@@ -303,11 +311,11 @@
         moved = dot_exact(jnp.where(pick, 1.0, 0.0), payload)
         for part in range(3):
             send_e[pl.ds(slot * 3 + part, n_cuts, stride=8), :] = moved[:, part * width:(part + 1) * width]
-    borrow = jnp.where(g == n_group - 1, n_cuts - 1, n_cuts)
+    carry_cut = jnp.where(jnp.logical_and(g >= n_group - 3, g <= n_group - 2), 1, 0)
 
     def to_cut(i):
-        k = (i + c) % n_cuts
-        push(9, tile(send_e, k), tile(recv_e, c), (k + borrow) % n_cuts, g)
+        k = wrap(i + c, n_cuts)
+        remote(9, tile(send_e, k), tile(recv_e, c), wrap(k + carry_cut, n_cuts), ahead_group).start()
 
     shape = (n_cuts, n_cuts)
     g_real = g.astype(F32)
@@ -348,7 +356,7 @@
             with tag("fwd%d" % h):
                 apply(cut_fwd, n_cuts, recv1.at[h], send2.at[h])
             def to_unit(i):
-                freq = (i + (3 * g) // 4) % n_cuts
+                freq = wrap(i + (3 * g) // 4, n_cuts)
                 u = 2 * freq + h
                 own = u < n_group
                 push(
@@ -365,11 +373,11 @@
         apply(mid_op, n_group, recv2, send3)
 
     for h in range(2):
-        @pl.when(unit % 2 == h)
+        @pl.when((unit & 1) == h)
         def _():
             def to_owner(i):
-                m = (i + g) % n_group
-                push(4 + h, tile(send3, m), tile(recv3.at[h], unit // 2), owner, m)
+                m = wrap(i + g, n_group)
+                push(4 + h, tile(send3, m), tile(recv3.at[h], unit >> 1), owner, m)
             with tag("send3"):
                 repeat(n_group, to_owner)
 
@@ -385,18 +393,16 @@
             with tag("inv%d" % h):
                 apply(cut_inv, n_cuts, recv3.at[h], send4.at[h])
             def to_slice(i):
-                k = (i + c) % n_cuts
+                k = wrap(i + c, n_cuts)
                 push(6 + h, tile(send4.at[h], k), tile(recv4.at[h], my_active), k, g)
             with tag("send4%d" % h):
                 repeat(n_cuts, to_slice)
 
     arrived(9, recv_e)
-    remote(10, recv_e, slip_e, *device(3)).start()
-    arrived(10, slip_e)
 
     def pieces(part):
         return jnp.concatenate(
-            [slip_e[pl.ds(part, n_cuts, stride=8), :], slip_e[pl.ds(3 + part, n_cuts, stride=8), :]], axis=0
+            [recv_e[pl.ds(part, n_cuts, stride=8), :], recv_e[pl.ds(3 + part, n_cuts, stride=8), :]], axis=0
         )
 
     def cells_of(value):
@@ -406,12 +412,12 @@
     slip_p[...] = cells
     remote(11, slip_p, got_p, *device(-1)).start()
     with tag("mark3"):
-        mark(many, cells_of(cells), hot_now, row_now)
+        mark(many, cells_of(cells), hot_now, row_now, turned_now)
     phase = pieces(0)
     cos, sin = jnp.cos(phase), jnp.sin(phase)
     arrived(11, got_p)
     with tag("mark4"):
-        mark(many, cells_of(got_p[...]), hot_next, row_next)
+        mark(many, cells_of(got_p[...]), hot_next, row_next, turned_next)
     for h in range(2):
         arrived(6 + h, recv4.at[h])
         for a in range(n_active):
@@ -427,7 +433,7 @@
         slip_b[many:] = power
     remote(12, slip_b, got_b, *device(-1)).start()
     with tag("deposit3"):
-        deposit(many, hot_now, row_now)
+        deposit(many, hot_now, row_now, turned_now)
     with tag("diffract3"):
         set_field(diffract(me != 1))
 
@@ -438,7 +444,7 @@
         phase = got_b[:many]
         kick(many, phase, got_b[many:], jnp.cos(phase), jnp.sin(phase))
     with tag("deposit4"):
-        deposit(many, hot_next, row_next)
+        deposit(many, hot_next, row_next, turned_next)
     with tag("diffract4"):
         result = diffract(me != 0)
         result_out[0] = result[:, :grid]
@@ -447,8 +453,7 @@
     store.start()
 
     sent(0, slip_a)
-    sent(9, send_e.at[pl.ds(0, (n_cuts - 1) * 8)])
-    sent(10, recv_e)
+    sent(9, send_e)
     sent(11, slip_p)
     sent(12, slip_b)
 
@@ -458,7 +463,7 @@
             sent(1 + h, send1.at[h, pl.ds(0, (n_active - 1) * 8)])
             sent(6 + h, send4.at[h, pl.ds(0, (n_cuts - 1) * 8)])
         for h in range(2):
-            @pl.when(unit % 2 == h)
+            @pl.when((unit & 1) == h)
             def _():
                 sent(4 + h, send3.at[pl.ds(0, (n_group - 1) * 8)])
         sent(3, send2.at[0])
@@ -468,7 +473,7 @@
     def _():
         for h in range(2):
             sent(1 + h, send1.at[h])
-            @pl.when(unit % 2 == h)
+            @pl.when((unit & 1) == h)
             def _():
                 sent(4 + h, send3)
     store.wait()
@@ -478,8 +483,6 @@
     grid = radiation.shape[-1]
     blocks, width = phases.shape[1:]
     many = 2 * n_cuts
-    chunk = 8 if many % 8 == 0 else many
-    marks = (many // chunk, 2 * grid, chunk * width)
     n_active = grid // ROWS
     vmem = lambda shape, kind=F32: pltpu.VMEM(shape, kind)
     scratch = [
@@ -490,10 +493,10 @@
         vmem((2 * n_cuts, 6 * n_cuts), BF16), vmem((2 * n_cuts, 6 * n_cuts), BF16),
         vmem((2 * n_group, 6 * n_group), BF16),
         vmem((3 * blocks + 8, width)), vmem((3 * blocks + 8, width)),
-        vmem((n_cuts * 8, width)),
         vmem((many, width)), vmem((many, width)),
         vmem((2 * many, width)), vmem((2 * many, width)),
-        vmem(marks, BF16), vmem(marks, BF16),
+        vmem((2 * grid, many * width), BF16), vmem((2 * grid, many * width), BF16),
+        vmem((many * width, 2 * grid), BF16), vmem((many * width, 2 * grid), BF16),
         vmem((many, width), jnp.int32), vmem((many, width), jnp.int32),
         vmem((2, many, width)), vmem((2, many, width)),
         vmem((grid, 2 * grid)),
@@ -507,11 +510,14 @@
     return pl.pallas_call(
         functools.partial(kernel, n_cuts, n_group, grid, blocks, width),
         out_shape=jax.ShapeDtypeStruct(radiation.shape, F32),
-        in_specs=[pl.BlockSpec(memory_space=pl.ANY)] * 7,
+        in_specs=[pl.BlockSpec(memory_space=pltpu.HBM)] * 7,
         out_specs=pl.BlockSpec(memory_space=pl.ANY),
         scratch_shapes=scratch,
-        compiler_params=pltpu.CompilerParams(collective_id=0, has_side_effects=True),
-    )(radiation, phases, energy, pixels, destination, propagator, transmit)
+        compiler_params=pltpu.CompilerParams(collective_id=0, has_side_effects=True, vmem_limit_bytes=32 << 20),
+    )(*(
+        pltpu.with_memory_space_constraint(x, pltpu.HBM)
+        for x in (radiation, phases, energy, pixels, destination, propagator, transmit)
+    ))
 
 
 def solution(mesh):

time: 72.8 us -> 66 us (0.907)
  Pallas kernels: 71.1 us -> 65.2 us
  local copies, waits for them, and re-layouts: 1.57 us -> 0.66 us
    pallas_call x1, Pallas kernels: 71.1 us -> 65.2 us  [on_device(): pl.pallas_call(functools.partial(kernel, n_cuts, n_group, grid, blocks, w...]
    unnamed x1, local copies, waits for them, and re-layouts: 1.57 us -> 0.66 us
where the time goes in v2:
time: 66 us; the launch traced here: 65.9 us
  Pallas kernels  65.2 us (99%)
  local copies, waits for them, and re-layouts  0.66 us (1%)
    pallas_call x1, Pallas kernels, on_device(): pl.pallas_call(functools.partial(kernel, n_cuts, n_group, grid, blocks, w...  65.2 us

profile of v2, /device:TPU:1, one launch (start us, length us, event | category | flops | bytes accessed | tf_op | source)
XLA Modules:
  0.0 65.9 jit_solution(16604347138336952803)
XLA Ops:
  0.0 65.2 %shard_map.73 = f32[1,2,128,128]{3,2,1,0:T(8,128)S(1)} custom-call(f32[1,2,128,128]{3,2,1,0:T(8,128)} %radiation.1, f32[1,16,128]{2,1,0:T(8,128)} %phases.1, f32[1,16,128]{2,1,0:T(8,128)} %energy.1, s32[1,16,128]{2,1,0:T(8,128)} %pixels.1, s32[1,16]{1,0:T(1,128)} %destination.1, f32[2,128,128]{2,1,0:T(8,128)} %propagator.1, f32[2,768]{1,0:T(2,128)} %transmit.1), custom_call_target="tpu_custom_call" | custom-call | tf_op jit(solution)/shard_map/pallas_call | solution.py:510
  65.2 0.7 copy.9

commit v3 on v2

--- a/solution.py
+++ b/solution.py
@@ -75,7 +75,7 @@
     slip_a, got_a, slip_p, got_p, slip_b, got_b,
     hot_now, hot_next, turned_now, turned_next, row_now, row_next, read, weight, source,
     send1, recv1, send2, recv2, send3, recv3, send4, recv4, send_e, recv_e,
-    load_sems, send_sems, recv_sems,
+    go_sem, load_sems, send_sems, recv_sems,
 ):
     c = lax.axis_index("cuts")
     g = lax.axis_index("group")
@@ -124,8 +124,12 @@
 
     ahead_group = wrap(g + 3, n_group)
     behind_group = wrap(g + n_group - 3, n_group)
-    ring = max(1, n_cuts // 2)
-    for j in sorted(range(n_cuts), key=lambda j: -min(j % ring, ring - j % ring)):
+    ring = n_cuts // 2
+    cut_order = sorted(range(n_cuts), key=lambda j: -min(j % ring, ring - j % ring))
+    quads = n_group // 4
+    quad_order = sorted(range(quads), key=lambda j: -min(j, quads - j))
+    quad = g // 4
+    for j in cut_order:
         cut = wrap(c + j, n_cuts)
         hello(cut, ahead_group)
         hello(cut, behind_group)
@@ -160,12 +164,13 @@
             device_id=(cc, gg), device_id_type=MESH,
         )
 
-    def push(stage, src, dst, cc, gg):
-        mine = jnp.logical_and(cc == c, gg == g)
-
+    def keep(stage, src, dst):
+        pltpu.make_async_copy(src, dst, recv_sems.at[stage]).start()
+
+    def push(mine, stage, src, dst, cc, gg):
         @pl.when(mine)
         def _():
-            pltpu.make_async_copy(src, dst, recv_sems.at[stage]).start()
+            keep(stage, src, dst)
 
         @pl.when(jnp.logical_not(mine))
         def _():
@@ -185,18 +190,25 @@
     pairs = grid // 2
     places = 2 * grid
 
-    def mark(count, cells, hot, rows, turned=None):
+    def low_rows(value, size):
+        packed = jnp.broadcast_to(value, (16, width)).astype(BF16)
+        return jnp.broadcast_to(packed[None], (size // 16, 16, width)).reshape(size, width)
+
+    def mark(count, cells, hot, rows, turned):
         rows[:count] = lax.shift_right_arithmetic(cells, shift)
-        place = cells & (places - 1)
+        place = (cells & (places - 1)).astype(F32)
+        spots = iota((places, width), 0).astype(F32).astype(BF16)
+        one, zero = jnp.ones((places, width), BF16), jnp.zeros((places, width), BF16)
         for b in range(count):
-            match = iota((places, width), 0) == jnp.broadcast_to(place[b:b + 1], (places, width))
-            hot[:, b * width:(b + 1) * width] = jnp.where(match, 1.0, 0.0).astype(BF16)
-        if turned is not None:
-            columns = jnp.transpose(place.astype(F32))
-            spot = iota((width, places), 1).astype(F32)
-            for b in range(count):
-                match = spot == jnp.broadcast_to(columns[:, b:b + 1], (width, places))
-                turned[b * width:(b + 1) * width] = jnp.where(match, 1.0, 0.0).astype(BF16)
+            hot[:, b * width:(b + 1) * width] = jnp.where(spots == low_rows(place[b:b + 1], places), one, zero)
+        columns = jnp.transpose(place)
+        spots = iota((width, grid), 1).astype(F32).astype(BF16)
+        one, zero = jnp.ones((width, grid), BF16), jnp.zeros((width, grid), BF16)
+        for b in range(count):
+            column = jnp.broadcast_to(columns[:, b:b + 1], (width, grid))
+            for q in range(2):
+                match = spots == (column - float(q * grid)).astype(BF16)
+                turned[b * width:(b + 1) * width, q * grid:(q + 1) * grid] = jnp.where(match, one, zero)
 
     def look(count, hot, rows):
         low = jnp.concatenate([field[pl.ds(0, grid, stride=2), :], field[pl.ds(1, grid, stride=2), :]], axis=1).astype(BF16)
@@ -219,22 +231,19 @@
         weight[1, :count] = -jnp.sin(phase)
         return phase, power
 
-    def deposit(count, hot, rows, turned=None):
+    def deposit(count, rows, turned):
         chunk = 8 if count % 8 == 0 else count
-        shape = (pairs, width)
         gathered = jnp.zeros((grid, places), F32)
+        spots = iota((pairs, width), 0).astype(F32).astype(BF16)
+        zero = jnp.zeros((pairs, width), BF16)
         for first in range(0, count, chunk):
             tops, bottoms = [], []
             for b in range(first, first + chunk):
-                match = iota(shape, 0) == jnp.broadcast_to(rows[b:b + 1], shape)
-                tops.append(jnp.where(match, jnp.broadcast_to(weight[0, b:b + 1], shape), 0.0).astype(BF16))
-                bottoms.append(jnp.where(match, jnp.broadcast_to(weight[1, b:b + 1], shape), 0.0).astype(BF16))
+                match = spots == low_rows(rows[b:b + 1].astype(F32), pairs)
+                tops.append(jnp.where(match, low_rows(weight[0, b:b + 1], pairs), zero))
+                bottoms.append(jnp.where(match, low_rows(weight[1, b:b + 1], pairs), zero))
             spread = jnp.concatenate([jnp.concatenate(tops, axis=1), jnp.concatenate(bottoms, axis=1)], axis=0)
-            span = slice(first * width, (first + chunk) * width)
-            if turned is None:
-                gathered = gathered + dot_nt(spread, hot[:, span])
-            else:
-                gathered = gathered + dot(spread, turned[span])
+            gathered = gathered + dot(spread, turned[first * width:(first + chunk) * width])
         source[...] = gathered
 
     def emit():
@@ -256,7 +265,7 @@
         field[grid:] = result[:, grid:]
 
     loads[0].wait()
-    mark(blocks, pixel_in[...], hot_now, row_now)
+    mark(blocks, pixel_in[...], hot_now, row_now, turned_now)
     for load in loads[1:]:
         load.wait()
     look(blocks, hot_now, row_now)
@@ -274,15 +283,15 @@
     high, low = split(prop)
     prop_hi[...] = high
     prop_lo[...] = low
-    deposit(blocks, hot_now, row_now)
+    deposit(blocks, row_now, turned_now)
     set_field(diffract(me != total - 1))
 
     arrived(0, got_a)
-    mark(blocks, got_a[2 * blocks:3 * blocks].astype(jnp.int32), hot_now, row_now)
+    mark(blocks, got_a[2 * blocks:3 * blocks].astype(jnp.int32), hot_now, row_now, turned_now)
     look(blocks, hot_now, row_now)
     phase = got_a[:blocks]
     phase, power = kick(blocks, phase, got_a[blocks:2 * blocks], jnp.cos(phase), jnp.sin(phase))
-    deposit(blocks, hot_now, row_now)
+    deposit(blocks, row_now, turned_now)
     result = diffract(me != total - 2)
     for a in range(n_active):
         for h in range(2):
@@ -290,11 +299,19 @@
             send1[h, a * 8:a * 8 + HALF] = result[at:at + HALF, :grid]
             send1[h, a * 8 + HALF:(a + 1) * 8] = result[at:at + HALF, grid:]
 
-    for h in range(2):
-        def to_active(i):
-            a = wrap(i + my_active, n_active)
-            push(1 + h, tile(send1.at[h], a), tile(recv1.at[h], c), 3 * (a >> 1) + 2 * (a & 1), g)
-        repeat(n_active, to_active)
+    for j in cut_order:
+        cut = wrap(c + j, n_cuts)
+        row = (cut * 43) >> 7
+        place = cut - 3 * row
+
+        @pl.when(place != 1)
+        def _():
+            a = 2 * row + (place >> 1)
+            for h in range(2):
+                if j:
+                    remote(1 + h, tile(send1.at[h], a), tile(recv1.at[h], c), cut, g).start()
+                else:
+                    keep(1 + h, tile(send1.at[h], a), tile(recv1.at[h], c))
 
     target = got_a[3 * blocks:3 * blocks + 1, :blocks]
     square = (blocks, blocks)
@@ -313,9 +330,11 @@
             send_e[pl.ds(slot * 3 + part, n_cuts, stride=8), :] = moved[:, part * width:(part + 1) * width]
     carry_cut = jnp.where(jnp.logical_and(g >= n_group - 3, g <= n_group - 2), 1, 0)
 
-    def to_cut(i):
-        k = wrap(i + c, n_cuts)
-        remote(9, tile(send_e, k), tile(recv_e, c), wrap(k + carry_cut, n_cuts), ahead_group).start()
+    def send_electrons():
+        for j in cut_order:
+            cut = wrap(c + j, n_cuts)
+            k = wrap(cut + n_cuts - carry_cut, n_cuts)
+            remote(9, tile(send_e, k), tile(recv_e, c), cut, ahead_group).start()
 
     shape = (n_cuts, n_cuts)
     g_real = g.astype(F32)
@@ -355,18 +374,35 @@
             arrived(1 + h, recv1.at[h])
             with tag("fwd%d" % h):
                 apply(cut_fwd, n_cuts, recv1.at[h], send2.at[h])
-            def to_unit(i):
-                freq = wrap(i + (3 * g) // 4, n_cuts)
-                u = 2 * freq + h
-                own = u < n_group
-                push(
-                    3, tile(send2.at[h], freq), tile(recv2, g),
-                    jnp.where(own, c, idle_cut), jnp.where(own, u, half_group * side + u - n_group),
-                )
-            with tag("send2%d" % h):
-                repeat(n_cuts, to_unit)
+        with tag("send2"):
+            for j in quad_order:
+                y = wrap(quad + j, quads)
+                for r in range(4):
+                    src, dst = tile(send2.at[r % 2], 2 * y + r // 2), tile(recv2, g)
+                    if j:
+                        remote(3, src, dst, c, 4 * y + r).start()
+                    else:
+                        push(4 * y + r == g, 3, src, dst, c, 4 * y + r)
+                low = y - side * (quads // 2)
+
+                @pl.when(jnp.logical_and(low >= 0, low < quads // 2))
+                def _():
+                    for r in range(4):
+                        src = tile(send2.at[r % 2], n_group // 2 + 2 * low + r // 2)
+                        remote(3, src, tile(recv2, g), idle_cut, 4 * y + r).start()
+
+        @pl.when(side == g // half_group)
+        def _():
+            pl.semaphore_signal(go_sem, inc=1, device_id=(idle_cut, g), device_id_type=MESH)
+
         with tag("sende"):
-            repeat(n_cuts, to_cut)
+            send_electrons()
+
+    @pl.when(idle)
+    def _():
+        with tag("go"):
+            pl.semaphore_wait(go_sem, 1)
+        send_electrons()
 
     arrived(3, recv2)
     with tag("mid"):
@@ -375,16 +411,15 @@
     for h in range(2):
         @pl.when((unit & 1) == h)
         def _():
-            def to_owner(i):
-                m = wrap(i + g, n_group)
-                push(4 + h, tile(send3, m), tile(recv3.at[h], unit >> 1), owner, m)
             with tag("send3"):
-                repeat(n_group, to_owner)
-
-    @pl.when(idle)
-    def _():
-        with tag("sende"):
-            repeat(n_cuts, to_cut)
+                for j in quad_order:
+                    y = wrap(quad + j, quads)
+                    for r in range(4):
+                        src, dst = tile(send3, 4 * y + r), tile(recv3.at[h], unit >> 1)
+                        if j:
+                            remote(4 + h, src, dst, owner, 4 * y + r).start()
+                        else:
+                            push(jnp.logical_and(active, 4 * y + r == g), 4 + h, src, dst, owner, 4 * y + r)
 
     @pl.when(active)
     def _():
@@ -392,11 +427,15 @@
             arrived(4 + h, recv3.at[h])
             with tag("inv%d" % h):
                 apply(cut_inv, n_cuts, recv3.at[h], send4.at[h])
-            def to_slice(i):
-                k = wrap(i + c, n_cuts)
-                push(6 + h, tile(send4.at[h], k), tile(recv4.at[h], my_active), k, g)
-            with tag("send4%d" % h):
-                repeat(n_cuts, to_slice)
+        with tag("send4"):
+            for j in cut_order:
+                cut = wrap(c + j, n_cuts)
+                for h in range(2):
+                    src, dst = tile(send4.at[h], cut), tile(recv4.at[h], my_active)
+                    if j:
+                        remote(6 + h, src, dst, cut, g).start()
+                    else:
+                        keep(6 + h, src, dst)
 
     arrived(9, recv_e)
 
@@ -433,7 +472,7 @@
         slip_b[many:] = power
     remote(12, slip_b, got_b, *device(-1)).start()
     with tag("deposit3"):
-        deposit(many, hot_now, row_now, turned_now)
+        deposit(many, row_now, turned_now)
     with tag("diffract3"):
         set_field(diffract(me != 1))
 
@@ -444,7 +483,7 @@
         phase = got_b[:many]
         kick(many, phase, got_b[many:], jnp.cos(phase), jnp.sin(phase))
     with tag("deposit4"):
-        deposit(many, hot_next, row_next, turned_next)
+        deposit(many, row_next, turned_next)
     with tag("diffract4"):
         result = diffract(me != 0)
         result_out[0] = result[:, :grid]
@@ -505,7 +544,7 @@
         vmem((n_group * 8, grid)), vmem((2, n_cuts * 8, grid)),
         vmem((2, n_cuts * 8, grid)), vmem((2, n_active * 8, grid)),
         vmem((n_cuts * 8, width)), vmem((n_cuts * 8, width)),
-        pltpu.SemaphoreType.DMA((8,)), pltpu.SemaphoreType.DMA((13,)), pltpu.SemaphoreType.DMA((13,)),
+        pltpu.SemaphoreType.REGULAR, pltpu.SemaphoreType.DMA((8,)), pltpu.SemaphoreType.DMA((13,)), pltpu.SemaphoreType.DMA((13,)),
     ]
     return pl.pallas_call(
         functools.partial(kernel, n_cuts, n_group, grid, blocks, width),

time: 66 us -> 63.9 us (0.968)
  Pallas kernels: 65.2 us -> 63.1 us
    pallas_call x1, Pallas kernels: 65.2 us -> 63.1 us  [on_device(): pl.pallas_call(functools.partial(kernel, n_cuts, n_group, grid, blocks, w...]
where the time goes in v3:
time: 63.9 us; the launch traced here: 63.7 us
  Pallas kernels  63.1 us (99%)
  local copies, waits for them, and re-layouts  0.66 us (1%)
    pallas_call x1, Pallas kernels, on_device(): pl.pallas_call(functools.partial(kernel, n_cuts, n_group, grid, blocks, w...  63.1 us

profile of v3, /device:TPU:1, one launch (start us, length us, event | category | flops | bytes accessed | tf_op | source)
XLA Modules:
  0.0 63.7 jit_solution(6114456241516500782)
XLA Ops:
  0.0 63.1 %shard_map.73 = f32[1,2,128,128]{3,2,1,0:T(8,128)S(1)} custom-call(f32[1,2,128,128]{3,2,1,0:T(8,128)} %radiation.1, f32[1,16,128]{2,1,0:T(8,128)} %phases.1, f32[1,16,128]{2,1,0:T(8,128)} %energy.1, s32[1,16,128]{2,1,0:T(8,128)} %pixels.1, s32[1,16]{1,0:T(1,128)} %destination.1, f32[2,128,128]{2,1,0:T(8,128)} %propagator.1, f32[2,768]{1,0:T(2,128)} %transmit.1), custom_call_target="tpu_custom_call" | custom-call | tf_op jit(solution)/shard_map/pallas_call | solution.py:549
  63.1 0.7 %copy.9 = f32[1,2,128,128]{3,2,1,0:T(8,128)} copy(f32[1,2,128,128]{3,2,1,0:T(8,128)S(1)} %shard_map.73) | data formatting | bytes 262144

commit v4 on v3

--- a/solution.py
+++ b/solution.py
@@ -70,11 +70,11 @@
     n_cuts, n_group, grid, blocks, width,
     radiation, phases, energy, pixels, destination, propagator, transmit,
     out,
-    phase_in, power_in, pixel_in, target_in, prop_in, gain_in, result_out,
+    phase_in, power_in, pixel_in, target_in, prop_in, gain_in,
     field, prop_hi, prop_lo, cut_fwd, cut_inv, mid_op,
     slip_a, got_a, slip_p, got_p, slip_b, got_b,
     hot_now, hot_next, turned_now, turned_next, row_now, row_next, read, weight, source,
-    send1, recv1, send2, recv2, send3, recv3, send4, recv4, send_e, recv_e,
+    send1, recv1, send2, recv2, send3, recv3, send4, recv4, send_e, recv_e, send_x, recv_x,
     go_sem, load_sems, send_sems, recv_sems,
 ):
     c = lax.axis_index("cuts")
@@ -183,8 +183,8 @@
     def sent(stage, ref):
         remote(stage, ref, ref, c, g).wait_send()
 
-    def tile(ref, index):
-        return ref.at[pl.ds(pl.multiple_of(index * 8, 8), 8)]
+    def tile(ref, index, rows=8):
+        return ref.at[pl.ds(pl.multiple_of(index * 8, 8), rows)]
 
     shift = grid.bit_length()
     pairs = grid // 2
@@ -322,19 +322,22 @@
     payload = jnp.concatenate([phase, power, got_a[2 * blocks:3 * blocks] + 1.0], axis=1)
     shape = (n_cuts, blocks)
     goes = jnp.broadcast_to(target, shape) == iota(shape, 0).astype(F32)
-    send_e[...] = jnp.zeros_like(send_e)
     for slot in range(2):
         pick = jnp.logical_and(goes, jnp.broadcast_to(rank, shape) == float(slot))
         moved = dot_exact(jnp.where(pick, 1.0, 0.0), payload)
-        for part in range(3):
-            send_e[pl.ds(slot * 3 + part, n_cuts, stride=8), :] = moved[:, part * width:(part + 1) * width]
+        for part in range(2):
+            send_e[pl.ds(slot * 2 + part, n_cuts, stride=8), :] = moved[:, part * width:(part + 1) * width]
+        send_x[pl.ds(slot, n_cuts, stride=8), :] = moved[:, 2 * width:]
     carry_cut = jnp.where(jnp.logical_and(g >= n_group - 3, g <= n_group - 2), 1, 0)
 
-    def send_electrons():
+    def send_electrons(stage, rows, src, dst):
         for j in cut_order:
             cut = wrap(c + j, n_cuts)
             k = wrap(cut + n_cuts - carry_cut, n_cuts)
-            remote(9, tile(send_e, k), tile(recv_e, c), cut, ahead_group).start()
+            remote(stage, tile(src, k, rows), tile(dst, c, rows), cut, ahead_group).start()
+
+    with tag("sendx"):
+        send_electrons(10, 2, send_x, recv_x)
 
     shape = (n_cuts, n_cuts)
     g_real = g.astype(F32)
@@ -391,18 +394,19 @@
                         src = tile(send2.at[r % 2], n_group // 2 + 2 * low + r // 2)
                         remote(3, src, tile(recv2, g), idle_cut, 4 * y + r).start()
 
+    @pl.when(active)
+    def _():
         @pl.when(side == g // half_group)
         def _():
             pl.semaphore_signal(go_sem, inc=1, device_id=(idle_cut, g), device_id_type=MESH)
-
-        with tag("sende"):
-            send_electrons()
 
     @pl.when(idle)
     def _():
         with tag("go"):
             pl.semaphore_wait(go_sem, 1)
-        send_electrons()
+
+    with tag("sende"):
+        send_electrons(9, 4, send_e, recv_e)
 
     arrived(3, recv2)
     with tag("mid"):
@@ -420,6 +424,17 @@
                             remote(4 + h, src, dst, owner, 4 * y + r).start()
                         else:
                             push(jnp.logical_and(active, 4 * y + r == g), 4 + h, src, dst, owner, 4 * y + r)
+
+    arrived(10, recv_x.at[pl.ds(0, n_cuts * 2)])
+
+    def cells_of(value):
+        return (value + 0.25).astype(jnp.int32) - 1
+
+    cells = jnp.concatenate([recv_x[pl.ds(0, n_cuts, stride=8), :], recv_x[pl.ds(1, n_cuts, stride=8), :]], axis=0)
+    slip_p[...] = cells
+    remote(11, slip_p, got_p, *device(-1)).start()
+    with tag("mark3"):
+        mark(many, cells_of(cells), hot_now, row_now, turned_now)
 
     @pl.when(active)
     def _():
@@ -437,26 +452,18 @@
                     else:
                         keep(6 + h, src, dst)
 
-    arrived(9, recv_e)
-
-    def pieces(part):
-        return jnp.concatenate(
-            [recv_e[pl.ds(part, n_cuts, stride=8), :], recv_e[pl.ds(3 + part, n_cuts, stride=8), :]], axis=0
-        )
-
-    def cells_of(value):
-        return (value + 0.25).astype(jnp.int32) - 1
-
-    cells = pieces(2)
-    slip_p[...] = cells
-    remote(11, slip_p, got_p, *device(-1)).start()
-    with tag("mark3"):
-        mark(many, cells_of(cells), hot_now, row_now, turned_now)
-    phase = pieces(0)
-    cos, sin = jnp.cos(phase), jnp.sin(phase)
     arrived(11, got_p)
     with tag("mark4"):
         mark(many, cells_of(got_p[...]), hot_next, row_next, turned_next)
+    arrived(9, recv_e.at[pl.ds(0, n_cuts * 4)])
+
+    def pieces(part):
+        return jnp.concatenate(
+            [recv_e[pl.ds(part, n_cuts, stride=8), :], recv_e[pl.ds(2 + part, n_cuts, stride=8), :]], axis=0
+        )
+
+    phase = pieces(0)
+    cos, sin = jnp.cos(phase), jnp.sin(phase)
     for h in range(2):
         arrived(6 + h, recv4.at[h])
         for a in range(n_active):
@@ -486,13 +493,12 @@
         deposit(many, row_next, turned_next)
     with tag("diffract4"):
         result = diffract(me != 0)
-        result_out[0] = result[:, :grid]
-        result_out[1] = result[:, grid:]
-    store = pltpu.make_async_copy(result_out, out.at[0], load_sems.at[0])
-    store.start()
+        out[0, 0] = result[:, :grid]
+        out[0, 1] = result[:, grid:]
 
     sent(0, slip_a)
-    sent(9, send_e)
+    sent(9, send_e.at[pl.ds(0, n_cuts * 4)])
+    sent(10, send_x.at[pl.ds(0, n_cuts * 2)])
     sent(11, slip_p)
     sent(12, slip_b)
 
@@ -515,7 +521,6 @@
             @pl.when((unit & 1) == h)
             def _():
                 sent(4 + h, send3)
-    store.wait()
 
 
 def on_device(n_cuts, n_group, radiation, phases, energy, pixels, destination, propagator, transmit):
@@ -526,7 +531,7 @@
     vmem = lambda shape, kind=F32: pltpu.VMEM(shape, kind)
     scratch = [
         vmem((blocks, width)), vmem((blocks, width)), vmem((blocks, width), jnp.int32),
-        vmem(destination.shape, jnp.int32), vmem(propagator.shape), vmem(transmit.shape), vmem(radiation.shape[1:]),
+        vmem(destination.shape, jnp.int32), vmem(propagator.shape), vmem(transmit.shape),
         vmem((2 * grid, grid)),
         vmem((2 * grid, 2 * grid), BF16), vmem((2 * grid, 2 * grid), BF16),
         vmem((2 * n_cuts, 6 * n_cuts), BF16), vmem((2 * n_cuts, 6 * n_cuts), BF16),
@@ -543,14 +548,14 @@
         vmem((2, n_cuts * 8, grid)), vmem((n_group * 8, grid)),
         vmem((n_group * 8, grid)), vmem((2, n_cuts * 8, grid)),
         vmem((2, n_cuts * 8, grid)), vmem((2, n_active * 8, grid)),
-        vmem((n_cuts * 8, width)), vmem((n_cuts * 8, width)),
+        vmem((n_cuts * 8, width)), vmem((n_cuts * 8, width)), vmem((n_cuts * 8, width)), vmem((n_cuts * 8, width)),
         pltpu.SemaphoreType.REGULAR, pltpu.SemaphoreType.DMA((8,)), pltpu.SemaphoreType.DMA((13,)), pltpu.SemaphoreType.DMA((13,)),
     ]
     return pl.pallas_call(
         functools.partial(kernel, n_cuts, n_group, grid, blocks, width),
         out_shape=jax.ShapeDtypeStruct(radiation.shape, F32),
         in_specs=[pl.BlockSpec(memory_space=pltpu.HBM)] * 7,
-        out_specs=pl.BlockSpec(memory_space=pl.ANY),
+        out_specs=pl.BlockSpec(memory_space=pltpu.VMEM),
         scratch_shapes=scratch,
         compiler_params=pltpu.CompilerParams(collective_id=0, has_side_effects=True, vmem_limit_bytes=32 << 20),
     )(*(

time: 63.9 us -> 64.1 us (level)
  no operation moved by 1% of the time
where the time goes in v4:
time: 64.1 us; the launch traced here: 64 us
  Pallas kernels  63.3 us (99%)
  local copies, waits for them, and re-layouts  0.66 us (1%)
    pallas_call x1, Pallas kernels, on_device(): pl.pallas_call(functools.partial(kernel, n_cuts, n_group, grid, blocks, w...  63.3 us

profile of v4, /device:TPU:1, one launch (start us, length us, event | category | flops | bytes accessed | tf_op | source)
XLA Modules:
  0.0 64.0 jit_solution(11857185611478567372)
XLA Ops:
  0.0 63.3 %shard_map.73 = f32[1,2,128,128]{3,2,1,0:T(8,128)S(1)} custom-call(f32[1,2,128,128]{3,2,1,0:T(8,128)} %radiation.1, f32[1,16,128]{2,1,0:T(8,128)} %phases.1, f32[1,16,128]{2,1,0:T(8,128)} %energy.1, s32[1,16,128]{2,1,0:T(8,128)} %pixels.1, s32[1,16]{1,0:T(1,128)} %destination.1, f32[2,128,128]{2,1,0:T(8,128)} %propagator.1, f32[2,768]{1,0:T(2,128)} %transmit.1), custom_call_target="tpu_custom_call" | custom-call | tf_op jit(solution)/shard_map/pallas_call | solution.py:554
  63.3 0.7 %copy.9 = f32[1,2,128,128]{3,2,1,0:T(8,128)} copy(f32[1,2,128,128]{3,2,1,0:T(8,128)S(1)} %shard_map.73) | data formatting | bytes 262144

commit v5 on v4

--- a/solution.py
+++ b/solution.py
@@ -190,6 +190,9 @@
     pairs = grid // 2
     places = 2 * grid
 
+    def alone(piece):
+        pl.when(me >= 0)(piece)
+
     def low_rows(value, size):
         packed = jnp.broadcast_to(value, (16, width)).astype(BF16)
         return jnp.broadcast_to(packed[None], (size // 16, 16, width)).reshape(size, width)
@@ -283,7 +286,7 @@
     high, low = split(prop)
     prop_hi[...] = high
     prop_lo[...] = low
-    deposit(blocks, row_now, turned_now)
+    alone(lambda: deposit(blocks, row_now, turned_now))
     set_field(diffract(me != total - 1))
 
     arrived(0, got_a)
@@ -291,7 +294,7 @@
     look(blocks, hot_now, row_now)
     phase = got_a[:blocks]
     phase, power = kick(blocks, phase, got_a[blocks:2 * blocks], jnp.cos(phase), jnp.sin(phase))
-    deposit(blocks, row_now, turned_now)
+    alone(lambda: deposit(blocks, row_now, turned_now))
     result = diffract(me != total - 2)
     for a in range(n_active):
         for h in range(2):
@@ -434,7 +437,7 @@
     slip_p[...] = cells
     remote(11, slip_p, got_p, *device(-1)).start()
     with tag("mark3"):
-        mark(many, cells_of(cells), hot_now, row_now, turned_now)
+        alone(lambda: mark(many, cells_of(slip_p[...]), hot_now, row_now, turned_now))
 
     @pl.when(active)
     def _():
@@ -454,7 +457,7 @@
 
     arrived(11, got_p)
     with tag("mark4"):
-        mark(many, cells_of(got_p[...]), hot_next, row_next, turned_next)
+        alone(lambda: mark(many, cells_of(got_p[...]), hot_next, row_next, turned_next))
     arrived(9, recv_e.at[pl.ds(0, n_cuts * 4)])
 
     def pieces(part):
@@ -472,25 +475,25 @@
             field[grid + at:grid + at + HALF] = recv4[h, a * 8 + HALF:(a + 1) * 8]
 
     with tag("look3"):
-        look(many, hot_now, row_now)
+        alone(lambda: look(many, hot_now, row_now))
     with tag("kick3"):
         phase, power = kick(many, phase, pieces(1), cos, sin)
         slip_b[:many] = phase
         slip_b[many:] = power
     remote(12, slip_b, got_b, *device(-1)).start()
     with tag("deposit3"):
-        deposit(many, row_now, turned_now)
+        alone(lambda: deposit(many, row_now, turned_now))
     with tag("diffract3"):
         set_field(diffract(me != 1))
 
     with tag("look4"):
-        look(many, hot_next, row_next)
+        alone(lambda: look(many, hot_next, row_next))
     arrived(12, got_b)
     with tag("kick4"):
         phase = got_b[:many]
         kick(many, phase, got_b[many:], jnp.cos(phase), jnp.sin(phase))
     with tag("deposit4"):
-        deposit(many, row_next, turned_next)
+        alone(lambda: deposit(many, row_next, turned_next))
     with tag("diffract4"):
         result = diffract(me != 0)
         out[0, 0] = result[:, :grid]

time: 64.1 us -> 63.6 us (level)
  no operation moved by 1% of the time
where the time goes in v5:
time: 63.6 us; the launch traced here: 63.5 us
  Pallas kernels  62.8 us (99%)
  local copies, waits for them, and re-layouts  0.66 us (1%)
    pallas_call x1, Pallas kernels, on_device(): pl.pallas_call(functools.partial(kernel, n_cuts, n_group, grid, blocks, w...  62.8 us

profile of v5, /device:TPU:1, one launch (start us, length us, event | category | flops | bytes accessed | tf_op | source)
XLA Modules:
  0.0 63.5 jit_solution(10825971630900412766)
XLA Ops:
  0.0 62.8 %shard_map.73 = f32[1,2,128,128]{3,2,1,0:T(8,128)S(1)} custom-call(f32[1,2,128,128]{3,2,1,0:T(8,128)} %radiation.1, f32[1,16,128]{2,1,0:T(8,128)} %phases.1, f32[1,16,128]{2,1,0:T(8,128)} %energy.1, s32[1,16,128]{2,1,0:T(8,128)} %pixels.1, s32[1,16]{1,0:T(1,128)} %destination.1, f32[2,128,128]{2,1,0:T(8,128)} %propagator.1, f32[2,768]{1,0:T(2,128)} %transmit.1), custom_call_target="tpu_custom_call" | custom-call | tf_op jit(solution)/shard_map/pallas_call | solution.py:557
  62.8 0.7 %copy.9 = f32[1,2,128,128]{3,2,1,0:T(8,128)} copy(f32[1,2,128,128]{3,2,1,0:T(8,128)S(1)} %shard_map.73) | data formatting | bytes 262144
